TPU v7x, 256 devices: a whole 4x4x8 slice. The times are simulated.
256 devices in a mesh: dp: 32 (over x, z), head: 8 (over y, core).
Axes of the slice: x: 4, y: 4, z: 8, core: 2. Of those that a mesh axis runs over, the one named last changes fastest.
Arguments:
- tokens: bfloat16 [16384, 4096], P('dp'), may hold values from -6 to 6
- q_weight: bfloat16 [4096, 8192], P('dp', 'head'), may hold values from -0.09375 to 0.09375
- kv_weight: bfloat16 [4096, 1024], P('dp', 'head'), may hold values from -0.09375 to 0.09375
- q_gain: float32 [128], replicated, may hold values from 0.1 to 1.9
- k_gain: float32 [128], replicated, may hold values from 0.1 to 1.9
- doc_lengths: int32 [32, 16], replicated, may hold values from 0 to 512, as said below
Outputs:
- attended: bfloat16 [16384, 8192], P('dp', 'head')
Inputs may be any that keep to these rules, and one draw needn't show every extreme that they name: `doc_lengths`: row r lists the lengths of the documents packed in order on index r of dp and sums to 512; some rank holds a single document of 512 tokens.
All inputs are finite; a program needn't handle non-finite values.
Results may differ from a plain program's by a relative error of at most 0.0068.
Values may be sent and summed in bfloat16 or wider, within the bound.
A program may use at most 64 MiB of HBM per device.

v0:
```python
import math
import jax
import jax.numpy as jnp
from jax import lax
from jax.sharding import PartitionSpec as P

KVH = 4
HD = 128
theta_base = 1000000.0
norm_eps = 1e-06


def doc_layout(lengths, count):
    doc_ends = jnp.cumsum(lengths)
    places = jnp.arange(count, dtype=jnp.int32)
    passed = (places[:, None] >= doc_ends[None, :]).astype(jnp.int32)
    doc_ids = jnp.sum(passed, axis=1)
    starts = jnp.sum(passed * lengths[None, :], axis=1)
    return (doc_ids, places - starts)


def norm_rope(raw, gain, positions):
    half_width = raw.shape[-1] // 2
    inv_rms = lax.rsqrt(jnp.mean(raw * raw, axis=-1, keepdims=True) + norm_eps)
    normed = raw * inv_rms * gain
    frequency = jnp.exp(
        jnp.arange(half_width, dtype=jnp.float32) * (-2.0 * math.log(theta_base) / raw.shape[-1])
    )
    angles = positions.astype(jnp.float32)[:, None] * frequency[None, :]
    cosine = jnp.cos(angles)[:, None, :]
    sine_table = jnp.sin(angles)[:, None, :]
    lower_half = normed[..., :half_width]
    second = normed[..., half_width:]
    return jnp.concatenate(
        [lower_half * cosine - second * sine_table, second * cosine + lower_half * sine_table],
        axis=-1,
    ).astype(jnp.bfloat16)


def shards(tokens, q_weight, kv_weight, q_gain, k_gain, doc_lengths):
    rows_here = tokens.shape[0]
    heads_here = q_weight.shape[1] // HD
    own_rank = lax.axis_index("dp")
    kv_all = lax.all_gather(kv_weight, "head", axis=1, tiled=True)
    kv_head = lax.axis_index("head") * KVH // lax.axis_size("head")
    key_cols = lax.dynamic_slice_in_dim(kv_all, kv_head * HD, HD, 1)
    value_cols = lax.dynamic_slice_in_dim(kv_all, (KVH + kv_head) * HD, HD, 1)
    pair_cols = jnp.concatenate([key_cols, value_cols], axis=1)

    def add_rows(shard_rows):
        return jnp.dot(tokens, shard_rows, preferred_element_type=jnp.float32)

    q_sum = add_rows(lax.all_gather(q_weight, "dp", axis=0, tiled=True))
    pair_sum = add_rows(lax.all_gather(pair_cols, "dp", axis=0, tiled=True))
    lengths = lax.dynamic_index_in_dim(doc_lengths, own_rank, 0, keepdims=False)
    doc_ids, positions = doc_layout(lengths, rows_here)
    places = jnp.arange(rows_here, dtype=jnp.int32)
    queries = norm_rope(q_sum.reshape(rows_here, heads_here, HD), q_gain, positions)
    key_rows = norm_rope(pair_sum[:, :HD].reshape(rows_here, 1, HD), k_gain, positions)[:, 0]
    values = pair_sum[:, HD:].astype(jnp.bfloat16)
    scores = jnp.einsum(
        "qhd,td->hqt", queries, key_rows, preferred_element_type=jnp.float32
    ) * HD ** (-0.5)
    allowed = (doc_ids[:, None] == doc_ids[None, :]) & (places[:, None] >= places[None, :])
    weights = jnp.where(allowed[None], jnp.exp(scores), 0.0)
    probs = (weights / jnp.sum(weights, axis=-1, keepdims=True)).astype(jnp.bfloat16)
    mixed_out = jnp.einsum("hqt,td->qhd", probs, values, preferred_element_type=jnp.float32)
    return mixed_out.astype(jnp.bfloat16).reshape(rows_here, heads_here * HD)


def solution(mesh):
    placed = (P("dp", None), P("dp", "head"), P("dp", "head"), P(), P(), P())
    return jax.shard_map(
        shards, mesh=mesh, in_specs=placed, out_specs=P("dp", "head"), check_vma=False
    )
```

profile of v0, /device:TPU:1, one launch (start us, length us, event | category | flops | bytes accessed | tf_op | source)
XLA Modules:
  0.0 222.3 jit_solution(3711025355796249315)
XLA Ops:
  6.5 14.7 %all_gather.9 = bf16[128,1024]{1,0:T(8,128)(2,1)S(1)} all-gather(bf16[128,128]{1,0:T(8,128)(2,1)} %param.8), channel_id=1, replica_groups=mesh['dp'=32,'head'=8] {'head'}, dimensions={1}, use_global_device_ids=true | all-gather | bytes 294912 | tf_op jit(solution)/shard_map/all_gather | solution.py:44
  21.3 0.6 pad_maximum_fusion
  22.0 0.0 all-gather.5.cloned.1.call-start
  22.0 0.7 all-gather.5.cloned.1.call-update
  22.7 0.9 dynamic-slice_reduce_fusion
  23.6 0.1 reduce.2
  23.8 0.1 convert_reduce_fusion
  23.9 0.9 fusion.8
  24.8 1.0 multiply_cosine_fusion
  25.8 70.1 %all-gather.3.cloned.1.call-done = bf16[4096,256]{1,0:T(8,128)(2,1)} async-done(((bf16[128,256]{1,0:T(8,128)(2,1)}), bf16[4096,256]{1,0:T(8,128)(2,1)}) %all-gather.3.cloned.1.call-update) | async-done | bytes 2097168 | tf_op jit(solution)/shard_map/all_gather | solution.py:54
  95.9 4.1 %convolution_bitcast_fusion = f32[512,256]{0,1:T(8,128)S(1)} fusion(bf16[4096,256]{1,0:T(8,128)(2,1)} %all-gather.3.cloned.1.call-done, bf16[512,4096]{1,0:T(8,128)(2,1)} %param.6), kind=kOutput, calls=%fused_computation.10 | convolution fusion | flops 1073741824 | bytes 6815744 | tf_op jit(solution)/shard_map/dot_general | solution.py:51
  100.1 0.1 multiply_bitcast_fusion
  100.2 0.6 fusion.22
  100.7 96.7 %all-gather.5.cloned.1.call-done = bf16[4096,1024]{1,0:T(8,128)(2,1)} async-done(((bf16[128,1024]{1,0:T(8,128)(2,1)}), bf16[4096,1024]{1,0:T(8,128)(2,1)}) %all-gather.5.cloned.1.call-update) | async-done | bytes 8388624 | tf_op jit(solution)/shard_map/all_gather | solution.py:53
  197.4 8.1 %fusion.26 = f32[512,1024]{1,0:T(8,128)S(1)} fusion(bf16[512,4096]{1,0:T(8,128)(2,1)} %param.6, bf16[4096,1024]{1,0:T(8,128)(2,1)} %all-gather.5.cloned.1.call-done), kind=kOutput, calls=%fused_computation.53 | convolution fusion | flops 4294967296 | bytes 14680064 | tf_op jit(solution)/shard_map/dot_general | solution.py:51
  205.6 0.5 copy.39
  206.1 0.6 multiply_reduce_fusion
  206.7 0.1 copy.30
  206.8 1.4 fusion.2
  208.2 0.8 subtract_convert_fusion
  209.0 0.2 copy-done
  209.1 2.6 %fusion = (f32[8,512]{1,0:T(8,128)S(1)}, f32[512,512,8]{1,0,2:T(8,128)S(1)}) fusion(pred[512,512]{0,1:T(8,128)(4,1)S(1)} %copy-done, bf16[512,8,64]{2,0,1:T(8,128)(2,1)S(1)} %get-tuple-element.8, bf16[512,8,64]{2,0,1:T(8,128)(2,1)S(1)} %get-tuple-element.7, bf16[512,64]{0,1:T(8,128)(2,1)S(1)} %get-tuple-element.10, bf16[512,64]{0,1:T(8,128)(2,1)S(1)} %get-tuple-element.9), kind=kOutput, calls=%fused_computation.2 | convolution fusion | flops 545517568 | bytes 9846784 | tf_op jit(solution)/shard_map/qhd,td->hqt/dot_general | solution.py:61
  211.7 2.4 %fusion.3 = bf16[128,8,512]{2,0,1:T(8,128)(2,1)S(1)} fusion(f32[512,512,8]{1,0,2:T(8,128)S(1)} %get-tuple-element.18, f32[8,512]{1,0:T(8,128)S(1)} %get-tuple-element.17, pred[512,512]{0,1:T(8,128)(4,1)S(1)} %copy-done, f32[512,256]{0,1:T(8,128)S(1)} %convolution_bitcast_fusion), kind=kOutput, calls=%fused_computation.9 | convolution fusion | flops 545783808 | bytes 9846784 | tf_op jit(solution)/shard_map/hqt,td->qhd/dot_general | solution.py:67
  214.1 1.3 copy.34
  (12 shorter events, 0.2 us)
Async XLA Ops:
  6.5 89.3 %all-gather.3.cloned.1.call-start = ((), (), s32[]{:S(2)}) async-start(), calls=%async_computation | async-start | bytes 2162688 | tf_op jit(solution)/shard_map/all_gather | solution.py:54
  22.0 175.5 %all-gather.5.cloned.1.call-start = ((), (), s32[]{:S(2)}) async-start(), calls=%async_computation.1 | async-start | bytes 8650752 | tf_op jit(solution)/shard_map/all_gather | solution.py:53
  25.8 74.3 %copy-start.1 = (f32[128]{0:T(128)S(1)}, f32[128]{0:T(128)}, u32[]{:S(2)}) copy-start(f32[128]{0:T(128)} %param.10) | copy-start | bytes 1540
  208.2 1.0 copy-start
Sparse Core Ops, SparseCore 0:
  22.1 73.7 all-gather.2
  98.5 98.9 all-gather.4
where the time goes:
time: 222 us
  waiting for transfers between devices  168 us (76%)
  matrix products  17.3 us (8%)
  blocking collectives  14.7 us (7%)
  between operations  13.5 us (6%)
  other arithmetic  6.22 us (3%)
  local copies, waits for them, and re-layouts  2.96 us (1%)
    all_gather x1, waiting for transfers between devices, shards(): q_sum = add_rows(lax.all_gather(q_weight, 'dp', axis=0, tiled=True))  96.7 us
    all_gather x1, waiting for transfers between devices, shards(): pair_sum = add_rows(lax.all_gather(pair_cols, 'dp', axis=0, tiled=True))  70.1 us
    all_gather x1, blocking collectives, shards(): kv_all = lax.all_gather(kv_weight, 'head', axis=1, tiled=True)  14.7 us
    dot_general x2, matrix products, add_rows(): return jnp.dot(tokens, shard_rows, preferred_element_type=jnp.float32)  12.3 us
  transfers between devices with their start and end apart: 2, of which 2 were waited for; matrix products, arithmetic and copies ran while one was open for 4% of the time, Pallas kernels for 0%

commit v1 on v0

--- a/solution.py
+++ b/solution.py
@@ -41,7 +41,8 @@
     rows_here = tokens.shape[0]
     heads_here = q_weight.shape[1] // HD
     own_rank = lax.axis_index("dp")
-    kv_all = lax.all_gather(kv_weight, "head", axis=1, tiled=True)
+    blocks = lax.all_gather(kv_weight, "head")
+    kv_all = jnp.concatenate(blocks, axis=1)
     kv_head = lax.axis_index("head") * KVH // lax.axis_size("head")
     key_cols = lax.dynamic_slice_in_dim(kv_all, kv_head * HD, HD, 1)
     value_cols = lax.dynamic_slice_in_dim(kv_all, (KVH + kv_head) * HD, HD, 1)

time: 222 us -> 223 us (level)
    all_gather x1, waiting for transfers between devices: 70.1 us -> 67.8 us  [shards(): pair_sum = add_rows(lax.all_gather(pair_cols, 'dp', axis=0, tiled=True))]
where the time goes in v1:
time: 223 us; the launch traced here: 222 us
  waiting for transfers between devices  166 us (74%)
  matrix products  17.2 us (8%)
  blocking collectives  16.1 us (7%)
  between operations  13.6 us (6%)
  other arithmetic  6.22 us (3%)
  local copies, waits for them, and re-layouts  3.13 us (1%)
    all_gather x1, waiting for transfers between devices, shards(): q_sum = add_rows(lax.all_gather(q_weight, 'dp', axis=0, tiled=True))  97.7 us
    all_gather x1, waiting for transfers between devices, shards(): pair_sum = add_rows(lax.all_gather(pair_cols, 'dp', axis=0, tiled=True))  67.8 us
    all_gather x1, blocking collectives, shards(): blocks = lax.all_gather(kv_weight, 'head')  16.1 us
    dot_general x2, matrix products, add_rows(): return jnp.dot(tokens, shard_rows, preferred_element_type=jnp.float32)  12.2 us
  transfers between devices with their start and end apart: 2, of which 2 were waited for; matrix products, arithmetic and copies ran while one was open for 4% of the time, Pallas kernels for 0%

profile of v1, /device:TPU:1, one launch (start us, length us, event | category | flops | bytes accessed | tf_op | source)
XLA Modules:
  0.0 222.5 jit_solution(8465692791971685948)
XLA Ops:
  6.5 16.1 %all-gather = bf16[1024,128]{1,0:T(8,128)(2,1)S(1)} all-gather(bf16[128,128]{1,0:T(8,128)(2,1)} %param.8), channel_id=2, replica_groups=mesh['dp'=32,'head'=8] {'head'}, dimensions={0}, use_global_device_ids=true | all-gather | bytes 294912 | tf_op jit(solution)/shard_map/all_gather | solution.py:44
  22.6 0.2 copy.37
  22.8 0.6 pad_maximum_fusion
  23.5 0.7 all-gather.6.cloned.1.call-update
  24.2 0.9 dynamic-slice_reduce_fusion
  25.1 0.1 reduce.2
  25.3 0.1 convert_reduce_fusion
  25.4 0.9 fusion.8
  26.3 1.0 multiply_cosine_fusion
  27.3 67.8 %all-gather.4.cloned.1.call-done = bf16[4096,256]{0,1:T(8,128)(2,1)} async-done(((bf16[128,256]{0,1:T(8,128)(2,1)}), bf16[4096,256]{0,1:T(8,128)(2,1)}) %all-gather.4.cloned.1.call-update) | async-done | bytes 2097168 | tf_op jit(solution)/shard_map/all_gather | solution.py:55
  95.1 4.1 %convolution_bitcast_fusion = f32[512,256]{0,1:T(8,128)S(1)} fusion(bf16[4096,256]{0,1:T(8,128)(2,1)} %all-gather.4.cloned.1.call-done, bf16[512,4096]{1,0:T(8,128)(2,1)} %param.6), kind=kOutput, calls=%fused_computation.10 | convolution fusion | flops 1073741824 | bytes 6815744 | tf_op jit(solution)/shard_map/dot_general | solution.py:52
  99.2 0.1 multiply_bitcast_fusion
  99.3 0.6 fusion.22
  99.9 97.7 %all-gather.6.cloned.1.call-done = bf16[4096,1024]{1,0:T(8,128)(2,1)} async-done(((bf16[128,1024]{1,0:T(8,128)(2,1)}), bf16[4096,1024]{1,0:T(8,128)(2,1)}) %all-gather.6.cloned.1.call-update) | async-done | bytes 8388624 | tf_op jit(solution)/shard_map/all_gather | solution.py:54
  197.6 8.1 %fusion.26 = f32[512,1024]{1,0:T(8,128)S(1)} fusion(bf16[512,4096]{1,0:T(8,128)(2,1)} %param.6, bf16[4096,1024]{1,0:T(8,128)(2,1)} %all-gather.6.cloned.1.call-done), kind=kOutput, calls=%fused_computation.53 | convolution fusion | flops 4294967296 | bytes 14680064 | tf_op jit(solution)/shard_map/dot_general | solution.py:52
  205.8 0.5 copy.48
  206.3 0.6 multiply_reduce_fusion
  206.9 0.1 copy.39
  207.0 1.4 fusion.2
  208.4 0.8 subtract_convert_fusion
  209.1 0.2 copy-done
  209.3 2.6 %fusion = (f32[8,512]{1,0:T(8,128)S(1)}, f32[512,512,8]{1,0,2:T(8,128)S(1)}) fusion(pred[512,512]{0,1:T(8,128)(4,1)S(1)} %copy-done, bf16[512,8,64]{2,0,1:T(8,128)(2,1)S(1)} %get-tuple-element.8, bf16[512,8,64]{2,0,1:T(8,128)(2,1)S(1)} %get-tuple-element.7, bf16[512,64]{0,1:T(8,128)(2,1)S(1)} %get-tuple-element.10, bf16[512,64]{0,1:T(8,128)(2,1)S(1)} %get-tuple-element.9), kind=kOutput, calls=%fused_computation.2 | convolution fusion | flops 545517568 | bytes 9846784 | tf_op jit(solution)/shard_map/qhd,td->hqt/dot_general | solution.py:62
  211.9 2.4 %fusion.3 = bf16[128,8,512]{2,0,1:T(8,128)(2,1)S(1)} fusion(f32[512,512,8]{1,0,2:T(8,128)S(1)} %get-tuple-element.18, f32[8,512]{1,0:T(8,128)S(1)} %get-tuple-element.17, pred[512,512]{0,1:T(8,128)(4,1)S(1)} %copy-done, f32[512,256]{0,1:T(8,128)S(1)} %convolution_bitcast_fusion), kind=kOutput, calls=%fused_computation.9 | convolution fusion | flops 545783808 | bytes 9846784 | tf_op jit(solution)/shard_map/hqt,td->qhd/dot_general | solution.py:68
  214.3 1.3 copy.43
  (13 shorter events, 0.2 us)
Async XLA Ops:
  6.5 88.5 %all-gather.4.cloned.1.call-start = ((), (), s32[]{:S(2)}) async-start(), calls=%async_computation | async-start | bytes 2162688 | tf_op jit(solution)/shard_map/all_gather | solution.py:55
  23.5 174.2 %all-gather.6.cloned.1.call-start = ((), (), s32[]{:S(2)}) async-start(), calls=%async_computation.1 | async-start | bytes 8650752 | tf_op jit(solution)/shard_map/all_gather | solution.py:54
  27.3 72.0 %copy-start.1 = (f32[128]{0:T(128)S(1)}, f32[128]{0:T(128)}, u32[]{:S(2)}) copy-start(f32[128]{0:T(128)} %param.10) | copy-start | bytes 1540
  208.4 1.0 copy-start
Sparse Core Ops, SparseCore 0:
  23.6 71.4 all-gather.3
  97.7 99.9 all-gather.5

commit v2 on v0

--- a/solution.py
+++ b/solution.py
@@ -8,6 +8,11 @@
 HD = 128
 theta_base = 1000000.0
 norm_eps = 1e-06
+
+
+def exchange_gather(value, axis, along):
+    sent = jnp.stack([value] * lax.axis_size(axis))
+    return jnp.concatenate(lax.all_to_all(sent, axis, 0, 0), axis=along)
 
 
 def doc_layout(lengths, count):
@@ -51,7 +56,7 @@
         return jnp.dot(tokens, shard_rows, preferred_element_type=jnp.float32)
 
     q_sum = add_rows(lax.all_gather(q_weight, "dp", axis=0, tiled=True))
-    pair_sum = add_rows(lax.all_gather(pair_cols, "dp", axis=0, tiled=True))
+    pair_sum = add_rows(exchange_gather(pair_cols, "dp", 0))
     lengths = lax.dynamic_index_in_dim(doc_lengths, own_rank, 0, keepdims=False)
     doc_ids, positions = doc_layout(lengths, rows_here)
     places = jnp.arange(rows_here, dtype=jnp.int32)

time: 222 us -> 154 us (0.69)
  waiting for transfers between devices: 168 us -> 89.2 us
  starting transfers between devices: 0.04 us -> 10.4 us
    all_gather x1 -> x0, waiting for transfers between devices: 70.1 us -> none  [shards(): pair_sum = add_rows(lax.all_gather(pair_cols, 'dp', axis=0, tiled=True))]
    all_gather x1, waiting for transfers between devices: 96.7 us -> 34.6 us  [shards(): q_sum = add_rows(lax.all_gather(q_weight, 'dp', axis=0, tiled=True))]
    all_to_all x0 -> x1, waiting for transfers between devices: none -> 53.9 us  [exchange_gather(): return jnp.concatenate(lax.all_to_all(sent, axis, 0, 0), axis=along)]
    all_to_all x0 -> x1, starting transfers between devices: none -> 10.4 us  [exchange_gather(): return jnp.concatenate(lax.all_to_all(sent, axis, 0, 0), axis=along)]
  transfers between devices with their start and end apart: 2 -> 2, of which waited for: 2 -> 2; matrix products, arithmetic and copies ran while one was open for 4% -> 5% of each run, Pallas kernels for 0% -> 0%
where the time goes in v2:
time: 154 us
  waiting for transfers between devices  89.2 us (58%)
  matrix products  16.8 us (11%)
  blocking collectives  14.8 us (10%)
  between operations  13.6 us (9%)
  starting transfers between devices  10.4 us (7%)
  other arithmetic  5.61 us (4%)
  local copies, waits for them, and re-layouts  3.88 us (3%)
    all_to_all x1, waiting for transfers between devices, exchange_gather(): return jnp.concatenate(lax.all_to_all(sent, axis, 0, 0), axis=along)  53.9 us
    all_gather x1, waiting for transfers between devices, shards(): q_sum = add_rows(lax.all_gather(q_weight, 'dp', axis=0, tiled=True))  34.6 us
    all_gather x1, blocking collectives, shards(): kv_all = lax.all_gather(kv_weight, 'head', axis=1, tiled=True)  14.8 us
    dot_general x2, matrix products, add_rows(): return jnp.dot(tokens, shard_rows, preferred_element_type=jnp.float32)  11.8 us
    all_to_all x1, starting transfers between devices, exchange_gather(): return jnp.concatenate(lax.all_to_all(sent, axis, 0, 0), axis=along)  10.4 us
  transfers between devices with their start and end apart: 2, of which 2 were waited for; matrix products, arithmetic and copies ran while one was open for 5% of the time, Pallas kernels for 0%

profile of v2, /device:TPU:1, one launch (start us, length us, event | category | flops | bytes accessed | tf_op | source)
XLA Modules:
  0.0 154.1 jit_solution(7735997187888704100)
XLA Ops:
  6.5 0.7 all-gather.2.cloned.1.call-update
  7.3 14.8 %all_gather.6 = bf16[128,1024]{1,0:T(8,128)(2,1)S(1)} all-gather(bf16[128,128]{1,0:T(8,128)(2,1)} %param.8), channel_id=1, replica_groups=mesh['dp'=32,'head'=8] {'head'}, dimensions={1}, use_global_device_ids=true | all-gather | bytes 294912 | tf_op jit(solution)/shard_map/all_gather | solution.py:49
  22.1 1.6 %stack.2 = bf16[32,128,256]{2,1,0:T(8,128)(2,1)} broadcast(bf16[128,256]{1,0:T(8,128)(2,1)S(1)} %pad_maximum_fusion), dimensions={1,2} | broadcast | bytes 2162688 | tf_op jit(solution)/shard_map/stack | solution.py:14
  23.7 10.4 %all-to-all-start = ((bf16[32,128,256]{2,1,0:T(8,128)(2,1)}), bf16[32,128,256]{2,1,0:T(8,128)(2,1)S(1)}, u32[]{:S(2)}, u32[]{:S(2)}) async-start(bf16[32,128,256]{2,1,0:T(8,128)(2,1)} %stack.2), calls=%async_computation | async-start | bytes 4194304 | tf_op jit(solution)/shard_map/all_to_all | solution.py:15
  34.1 0.2 dynamic-slice_reduce_fusion
  34.3 0.1 reduce.2
  34.4 0.1 convert_reduce_fusion
  34.6 0.9 fusion.8
  35.5 1.0 multiply_cosine_fusion
  36.5 53.9 %all-to-all-done = bf16[32,128,256]{2,1,0:T(8,128)(2,1)S(1)} async-done(((bf16[32,128,256]{2,1,0:T(8,128)(2,1)}), bf16[32,128,256]{2,1,0:T(8,128)(2,1)S(1)}, u32[]{:S(2)}, u32[]{:S(2)}) %all-to-all-start) | async-done | bytes 2097184 | tf_op jit(solution)/shard_map/all_to_all | solution.py:15
  90.3 3.6 %convolution_bitcast_fusion = f32[512,256]{0,1:T(8,128)S(1)} fusion(bf16[4096,256]{1,0:T(8,128)(2,1)S(1)} %bitcast.46, bf16[512,4096]{1,0:T(8,128)(2,1)} %param.6), kind=kOutput, calls=%fused_computation.10 | convolution fusion | flops 1073741824 | bytes 6815744 | tf_op jit(solution)/shard_map/dot_general | solution.py:56
  94.0 0.1 multiply_bitcast_fusion
  94.1 0.6 fusion.22
  94.7 34.6 %all-gather.2.cloned.1.call-done = bf16[4096,1024]{1,0:T(8,128)(2,1)} async-done(((bf16[128,1024]{1,0:T(8,128)(2,1)}), bf16[4096,1024]{1,0:T(8,128)(2,1)}) %all-gather.2.cloned.1.call-update) | async-done | bytes 8388624 | tf_op jit(solution)/shard_map/all_gather | solution.py:58
  129.3 8.1 %fusion.26 = f32[512,1024]{1,0:T(8,128)S(1)} fusion(bf16[512,4096]{1,0:T(8,128)(2,1)} %param.6, bf16[4096,1024]{1,0:T(8,128)(2,1)} %all-gather.2.cloned.1.call-done), kind=kOutput, calls=%fused_computation.53 | convolution fusion | flops 4294967296 | bytes 14680064 | tf_op jit(solution)/shard_map/dot_general | solution.py:56
  137.4 0.5 copy.39
  137.9 0.6 multiply_reduce_fusion
  138.5 0.1 copy.30
  138.6 1.4 fusion.2
  140.0 0.8 subtract_convert_fusion
  140.8 0.2 copy-done
  140.9 2.6 %fusion = (f32[8,512]{1,0:T(8,128)S(1)}, f32[512,512,8]{1,0,2:T(8,128)S(1)}) fusion(pred[512,512]{0,1:T(8,128)(4,1)S(1)} %copy-done, bf16[512,8,64]{2,0,1:T(8,128)(2,1)S(1)} %get-tuple-element.8, bf16[512,8,64]{2,0,1:T(8,128)(2,1)S(1)} %get-tuple-element.7, bf16[512,64]{0,1:T(8,128)(2,1)S(1)} %get-tuple-element.10, bf16[512,64]{0,1:T(8,128)(2,1)S(1)} %get-tuple-element.9), kind=kOutput, calls=%fused_computation.2 | convolution fusion | flops 545517568 | bytes 9846784 | tf_op jit(solution)/shard_map/qhd,td->hqt/dot_general | solution.py:66
  143.6 2.4 %fusion.3 = bf16[128,8,512]{2,0,1:T(8,128)(2,1)S(1)} fusion(f32[512,512,8]{1,0,2:T(8,128)S(1)} %get-tuple-element.18, f32[8,512]{1,0:T(8,128)S(1)} %get-tuple-element.17, pred[512,512]{0,1:T(8,128)(4,1)S(1)} %copy-done, f32[512,256]{0,1:T(8,128)S(1)} %convolution_bitcast_fusion), kind=kOutput, calls=%fused_computation.9 | convolution fusion | flops 545783808 | bytes 9846784 | tf_op jit(solution)/shard_map/hqt,td->qhd/dot_general | solution.py:72
  146.0 1.3 copy.34
  (14 shorter events, 0.2 us)
Async XLA Ops:
  6.5 122.7 %all-gather.2.cloned.1.call-start = ((), (), s32[]{:S(2)}) async-start(), calls=%async_computation.1 | async-start | bytes 8650752 | tf_op jit(solution)/shard_map/all_gather | solution.py:58
  23.7 10.4 %copy-start.1 = (s32[32,16]{0,1:T(8,128)S(1)}, s32[32,16]{0,1:T(8,128)}, u32[]{:S(2)}) copy-start(s32[32,16]{0,1:T(8,128)} %param.11) | copy-start | bytes 6148
  23.7 66.6 %all-to-all-start = ((bf16[32,128,256]{2,1,0:T(8,128)(2,1)}), bf16[32,128,256]{2,1,0:T(8,128)(2,1)S(1)}, u32[]{:S(2)}, u32[]{:S(2)}) async-start(bf16[32,128,256]{2,1,0:T(8,128)(2,1)} %stack.2), calls=%async_computation | async-start | bytes 4194304 | tf_op jit(solution)/shard_map/all_to_all | solution.py:15
  90.3 3.7 %copy-start.2 = (f32[128]{0:T(128)S(1)}, f32[128]{0:T(128)}, u32[]{:S(2)}) copy-start(f32[128]{0:T(128)} %param.10) | copy-start | bytes 1540
  140.0 1.0 copy-start
Sparse Core Ops, SparseCore 0:
  9.9 119.2 all-gather.1
